TPU v7x, 32 devices: a whole 2x2x4 slice. The times are simulated.
32 devices in a mesh: cases: 2 (over x), box: 16 (over z, y, core).
Axes of the slice: x: 2, y: 2, z: 4, core: 2. Of those that a mesh axis runs over, the one named last changes fastest.
Arguments:
- positions: float32 [2048, 3, 128], P(('cases', 'box')), parts along dimension 0, may hold values from -9 to 9, as said below
- strengths: float32 [2048, 3, 128], P(('cases', 'box')), parts along dimension 0, may hold values from -12 to 12
- history: float32 [2048, 2, 3, 128], P(('cases', 'box')), parts along dimension 0, may hold values from -5 to 5
- move_list: int32 [2048], P(('cases', 'box')), parts along dimension 0, may hold values from 0 to 1023, as said below
- age_slot: int32 [2048], P(('cases', 'box')), parts along dimension 0, may hold values from 0 to 1023, as said below
- fetch_list: int32 [32, 16, 8], P(('cases', 'box')), parts along dimension 0, may hold values from -1 to 63, as said below
- tile_slot: int32 [2048, 32], P(('cases', 'box')), parts along dimension 0, may hold values from 0 to 127, as said below
- tile_count: int32 [2048], P(('cases', 'box')), parts along dimension 0, may hold values from 1 to 32, as said below
- blade_id: int32 [2048, 128], P(('cases', 'box')), parts along dimension 0, may hold values from 0 to 17
- hub_centre: float32 [12, 3], P('cases'), parts along dimension 0, may hold values from -8 to 8
- azimuth: float32 [12], P('cases'), parts along dimension 0, may hold values from -3.140625 to 3.140625
Outputs:
- new_positions: float32 [2048, 3, 128], P(('cases', 'box')), parts along dimension 0
- new_history: float32 [2048, 2, 3, 128], P(('cases', 'box')), parts along dimension 0
- frame: float32 [2048, 3, 128], P(('cases', 'box')), parts along dimension 0
There are 2 independent parts, one for each index of `cases`. A program takes and returns all parts, laid end to end along the dimension named above; each array names one. Nothing has to cross between parts.
Inputs may be any that keep to these rules, and one draw needn't show every extreme that they name: Node positions; the first component of a block's nodes is offset by an amount that grows with the block's device. `move_list`: A permutation of block ids (block id = device * 64 + local block). Each device receives 64 blocks; the blocks of one device go at most 8 to any one device, and every device sends exactly 8 to some device. `age_slot`: A permutation of block ids, with the same bounds per pair of devices as move_list. `fetch_list`: entry [r, o, i] is -1 or a local block of device o; live entries come first in each [r, o] row and are distinct; rows [r, o] with o within two of r around the axis have 8 live entries. `tile_slot`: every entry names a live entry of fetch_list for the target block's device; tiles may repeat. `tile_count`: the first block of each device has 32.
All inputs are finite; a program needn't handle non-finite values.
Results may differ from a plain program's by a relative error of at most 0.0003.
Values sent between devices are 32-bit elements; how exact they have to be, the bound alone decides.
No kernel may reach another device: no remote copies, remote signals or barrier semaphores. Data moves between devices by JAX's collectives and lax.ppermute only.
A program may use at most 128 MiB of HBM per device.

v0:
```python
import math
import jax
import jax.numpy as jnp
from jax import lax
from jax.sharding import PartitionSpec as P

ROTORS = 6
BLADES = 3
core_square = 0.05
time_step = 0.05


def cross_product(first, second):
    return jnp.stack(
        [
            first[..., 1, :] * second[..., 2, :] - first[..., 2, :] * second[..., 1, :],
            first[..., 2, :] * second[..., 0, :] - first[..., 0, :] * second[..., 2, :],
            first[..., 0, :] * second[..., 1, :] - first[..., 1, :] * second[..., 0, :],
        ],
        axis=-2,
    )


def induced(target, source_pos, source_table, tile_mask):
    dist_sq = jnp.zeros((source_pos.shape[0], target.shape[-1], source_pos.shape[-1]), jnp.float32)
    for component in range(3):
        gap = target[component][None, :, None] - source_pos[:, component][:, None, :]
        dist_sq = dist_sq + gap * gap
    weight = tile_mask[:, None, None] * (dist_sq + core_square) ** (-1.5)
    summed = jnp.einsum("kij,kcj->ci", weight, source_table, precision=lax.Precision.HIGHEST)
    return (cross_product(target, summed[:3]) - summed[3:]) / (4.0 * math.pi)


def pack_blocks(values, targets, blocks, box_count, capacity):
    dest_box = targets // blocks
    dest_local = targets % blocks
    one_hot = (dest_box[:, None] == jnp.arange(box_count, dtype=jnp.int32)[None, :]).astype(
        jnp.int32
    )
    earlier = jnp.cumsum(one_hot, axis=0) - one_hot
    ranking = jnp.sum(earlier * one_hot, axis=1)
    place = dest_box * capacity + ranking
    buffer = (
        jnp.zeros((box_count * capacity,) + values.shape[1:], values.dtype).at[place].set(values)
    )
    labels = (
        jnp.full((box_count * capacity,), -1.0, jnp.float32)
        .at[place]
        .set(dest_local.astype(jnp.float32))
    )
    return (buffer, labels)


def unpack_blocks(arrived, labels, blocks):
    place = jnp.where(labels >= 0.0, labels, float(blocks)).astype(jnp.int32)
    return (
        jnp.zeros((blocks,) + arrived.shape[1:], arrived.dtype).at[place].set(arrived, mode="drop")
    )


def body(
    positions,
    strengths,
    history,
    move_list,
    age_slot,
    fetch_list,
    tile_slot,
    tile_count,
    blade_id,
    hub_centre,
    azimuth,
):
    blocks = positions.shape[0]
    box_count = lax.axis_size("box")
    capacity = 2 * blocks // box_count
    offered = jnp.concatenate([positions, strengths], axis=1)
    requests = fetch_list[0]
    everything = lax.all_gather(offered, "box", axis=0, tiled=True)
    wanted = jnp.arange(box_count, dtype=jnp.int32)[:, None] * blocks + jnp.clip(
        requests, 0, blocks - 1
    )
    fetched = jnp.take(everything, wanted.reshape(-1), axis=0)
    source_pos = fetched[:, :3]
    source_table = jnp.concatenate(
        [fetched[:, 3:], cross_product(fetched[:, :3], fetched[:, 3:])], axis=1
    )
    tile_mask = (
        jnp.arange(tile_slot.shape[1], dtype=jnp.int32)[None, :] < tile_count[:, None]
    ).astype(jnp.float32)

    def one_target(packed):
        target, slots, weights = packed
        return induced(
            target,
            jnp.take(source_pos, slots, axis=0),
            jnp.take(source_table, slots, axis=0),
            weights,
        )

    velocity = lax.map(one_target, (positions, tile_slot, tile_mask), batch_size=4)
    buffer, labels = pack_blocks(history, move_list, blocks, box_count, capacity)
    arrived, arrived_labels = (
        lax.all_to_all(buffer, "box", split_axis=0, concat_axis=0, tiled=True),
        lax.all_to_all(labels, "box", split_axis=0, concat_axis=0, tiled=True),
    )
    moved = unpack_blocks(arrived, arrived_labels, blocks)
    new_positions = (
        positions + time_step * (23.0 * velocity - 16.0 * moved[:, 0] + 5.0 * moved[:, 1]) / 12.0
    )
    new_history = jnp.stack([velocity, moved[:, 0]], axis=1)
    age_buffer, age_labels = pack_blocks(new_positions, age_slot, blocks, box_count, capacity)
    aged_in, aged_labels = (
        lax.all_to_all(age_buffer, "box", split_axis=0, concat_axis=0, tiled=True),
        lax.all_to_all(age_labels, "box", split_axis=0, concat_axis=0, tiled=True),
    )
    aged = unpack_blocks(aged_in, aged_labels, blocks)
    classes = ROTORS * BLADES
    blade_angle = (
        azimuth[:, None] + 2.0 * math.pi * jnp.arange(BLADES, dtype=jnp.float32)[None, :] / BLADES
    ).reshape(-1)
    centre_table = jnp.repeat(hub_centre, BLADES, axis=0)
    selector = (blade_id[None, :, :] == jnp.arange(classes, dtype=jnp.int32)[:, None, None]).astype(
        jnp.float32
    )
    cosine = jnp.sum(selector * jnp.cos(blade_angle)[:, None, None], axis=0)
    sine = jnp.sum(selector * jnp.sin(blade_angle)[:, None, None], axis=0)
    first = aged[:, 0] - jnp.sum(selector * centre_table[:, 0][:, None, None], axis=0)
    second = aged[:, 1] - jnp.sum(selector * centre_table[:, 1][:, None, None], axis=0)
    third = aged[:, 2] - jnp.sum(selector * centre_table[:, 2][:, None, None], axis=0)
    frame = jnp.stack(
        [cosine * first + sine * second, cosine * second - sine * first, third], axis=1
    )
    return (new_positions, new_history, frame)


def solution(mesh):
    placed = (
        P(("cases", "box"), None, None),
        P(("cases", "box"), None, None),
        P(("cases", "box"), None, None, None),
        P(("cases", "box")),
        P(("cases", "box")),
        P(("cases", "box"), None, None),
        P(("cases", "box"), None),
        P(("cases", "box")),
        P(("cases", "box"), None),
        P("cases", None),
        P("cases"),
    )
    return jax.shard_map(
        body,
        mesh=mesh,
        in_specs=placed,
        out_specs=(
            P(("cases", "box"), None, None),
            P(("cases", "box"), None, None, None),
            P(("cases", "box"), None, None),
        ),
        check_vma=False,
    )
```

profile of v0, /device:TPU:0, one launch (start us, length us, event | category | flops | bytes accessed | tf_op | source)
XLA Modules:
  0.0 342.8 jit_solution(4448846752251217391)
XLA Ops:
  7.2 1.6 pad_maximum_fusion.1
  11.4 7.4 %all-to-all-start = ((f32[16,8,1]{1,2,0:T(1,128)}), f32[16,8,1]{1,2,0:T(1,128)S(1)}, u32[]{:S(2)}, u32[]{:S(2)}) async-start(f32[16,8,1]{1,2,0:T(1,128)} %bitcast.25), calls=%async_computation | async-start | bytes 16384 | tf_op jit(solution)/shard_map/all_to_all | solution.py:105
  25.8 0.8 broadcast_in_dim.87
  26.7 8.0 %scatter_fusion = f32[128,2,3,128]{3,1,2,0:T(2,128)} fusion(f32[128,2,3,128]{3,1,2,0:T(2,128)} %broadcast_in_dim.87, s32[64]{0:T(128)S(1)} %compare_select_fusion.7, f32[64,2,3,128]{3,1,2,0:T(2,128)} %param.15), kind=kCustom, calls=%fused_computation.4 | custom fusion | bytes 590080 | tf_op jit(solution)/shard_map/scatter | solution.py:44
  34.7 6.0 %all-to-all-start.1 = ((f32[128,2,3,128]{3,1,2,0:T(2,128)}), f32[128,2,3,128]{3,1,2,0:T(2,128)S(1)}, u32[]{:S(2)}, u32[]{:S(2)}) async-start(f32[128,2,3,128]{3,1,2,0:T(2,128)} %scatter_fusion), calls=%async_computation.1 | async-start | bytes 786432 | tf_op jit(solution)/shard_map/all_to_all | solution.py:104
  42.1 17.4 %all-to-all-done.1 = f32[128,2,3,128]{3,1,2,0:T(2,128)S(1)} async-done(((f32[128,2,3,128]{3,1,2,0:T(2,128)}), f32[128,2,3,128]{3,1,2,0:T(2,128)S(1)}, u32[]{:S(2)}, u32[]{:S(2)}) %all-to-all-start.1) | async-done | bytes 393248 | tf_op jit(solution)/shard_map/all_to_all | solution.py:104
  59.5 6.2 %all-to-all-start.2 = ((f32[16,8,1]{1,2,0:T(1,128)}), f32[16,8,1]{1,2,0:T(1,128)S(1)}, u32[]{:S(2)}, u32[]{:S(2)}) async-start(f32[16,8,1]{1,2,0:T(1,128)} %bitcast.31), calls=%async_computation.2 | async-start | bytes 16384 | tf_op jit(solution)/shard_map/all_to_all | solution.py:115
  65.8 4.7 %scatter_fusion.1 = f32[64,2,3,128]{3,1,2,0:T(2,128)S(1)} fusion(f32[64,2,3,128]{3,1,2,0:T(2,128)S(1)} %broadcast_in_dim.84, s32[128]{0:T(128)S(1)} %fusion.44, f32[128,2,3,128]{3,1,2,0:T(2,128)S(1)} %all-to-all-done.1), kind=kCustom, calls=%fused_computation.5 | custom fusion | bytes 1180160 | tf_op jit(solution)/shard_map/scatter | solution.py:57
  70.7 5.7 %copy.106 = f32[1024,6,128]{2,1,0:T(8,128)} copy(f32[1024,6,128]{2,0,1:T(8,128)} %all-gather.2.cloned.1.call-done) | data formatting | bytes 6291456 | tf_op jit(solution)/shard_map/all_gather | solution.py:79
  76.4 2.9 gather_fusion.2
  80.2 226.8 %while.10 = (s32[]{:T(128)}, f32[16,4,3,128]{3,2,1,0:T(4,128)S(1)}, f32[16,4,3,128]{3,1,0,2:T(4,128)S(1)}, s32[16,4,32]{2,1,0:T(4,128)S(1)}, f32[128,6,128]{2,1,...) while((s32[]{:T(128)}, f32[16,4,3,128]{3,2,1,0:T(4,128)S(1)}, ...), condition=%wide.region_1.2_spmd, body=%wide.region_0.1_spmd.sunk | while | flops 172126848 | bytes 2662377 | solution.py:101
  82.4 12.0 %fusion.64 = f32[4,6,128]{2,1,0:T(8,128)S(1)} fusion(f32[4,32,128]{2,1,0:T(8,128)S(1)} %bitcast.126, f32[4,128]{1,0:T(4,128)S(1)} %get-tuple-element.200, f32[4,32,128]{2,1,0:T(8,128)S(1)} %bitcast.127, f32[4,128]{1,0:T(4,128)S(1)} %get-tuple-element.202, f32[4,32,128]{2,1,0:T(8,128)S(1)} %bitcast.125, f32[4,128]{1,0:T(4,128)S(1)} %get-tuple-element.204, ...), kind=kOutput, calls=%fused_computation.30.clone.1 | convolution fusion | flops 172064768 | bytes 608896 | tf_op jit(solution)/shard_map/while/body/eval_jaxpr/vmap(kij,kcj->ci)/dot_general | solution.py:30
  96.6 12.0 %fusion.64 = f32[4,6,128]{2,1,0:T(8,128)S(1)} fusion(f32[4,32,128]{2,1,0:T(8,128)S(1)} %bitcast.126, f32[4,128]{1,0:T(4,128)S(1)} %get-tuple-element.200, f32[4,32,128]{2,1,0:T(8,128)S(1)} %bitcast.127, f32[4,128]{1,0:T(4,128)S(1)} %get-tuple-element.202, f32[4,32,128]{2,1,0:T(8,128)S(1)} %bitcast.125, f32[4,128]{1,0:T(4,128)S(1)} %get-tuple-element.204, ...), kind=kOutput, calls=%fused_computation.30.clone.1 | convolution fusion | flops 172064768 | bytes 608896 | tf_op jit(solution)/shard_map/while/body/eval_jaxpr/vmap(kij,kcj->ci)/dot_general | solution.py:30
  110.8 12.0 %fusion.64 = f32[4,6,128]{2,1,0:T(8,128)S(1)} fusion(f32[4,32,128]{2,1,0:T(8,128)S(1)} %bitcast.126, f32[4,128]{1,0:T(4,128)S(1)} %get-tuple-element.200, f32[4,32,128]{2,1,0:T(8,128)S(1)} %bitcast.127, f32[4,128]{1,0:T(4,128)S(1)} %get-tuple-element.202, f32[4,32,128]{2,1,0:T(8,128)S(1)} %bitcast.125, f32[4,128]{1,0:T(4,128)S(1)} %get-tuple-element.204, ...), kind=kOutput, calls=%fused_computation.30.clone.1 | convolution fusion | flops 172064768 | bytes 608896 | tf_op jit(solution)/shard_map/while/body/eval_jaxpr/vmap(kij,kcj->ci)/dot_general | solution.py:30
  124.9 12.0 %fusion.64 = f32[4,6,128]{2,1,0:T(8,128)S(1)} fusion(f32[4,32,128]{2,1,0:T(8,128)S(1)} %bitcast.126, f32[4,128]{1,0:T(4,128)S(1)} %get-tuple-element.200, f32[4,32,128]{2,1,0:T(8,128)S(1)} %bitcast.127, f32[4,128]{1,0:T(4,128)S(1)} %get-tuple-element.202, f32[4,32,128]{2,1,0:T(8,128)S(1)} %bitcast.125, f32[4,128]{1,0:T(4,128)S(1)} %get-tuple-element.204, ...), kind=kOutput, calls=%fused_computation.30.clone.1 | convolution fusion | flops 172064768 | bytes 608896 | tf_op jit(solution)/shard_map/while/body/eval_jaxpr/vmap(kij,kcj->ci)/dot_general | solution.py:30
  139.1 12.0 %fusion.64 = f32[4,6,128]{2,1,0:T(8,128)S(1)} fusion(f32[4,32,128]{2,1,0:T(8,128)S(1)} %bitcast.126, f32[4,128]{1,0:T(4,128)S(1)} %get-tuple-element.200, f32[4,32,128]{2,1,0:T(8,128)S(1)} %bitcast.127, f32[4,128]{1,0:T(4,128)S(1)} %get-tuple-element.202, f32[4,32,128]{2,1,0:T(8,128)S(1)} %bitcast.125, f32[4,128]{1,0:T(4,128)S(1)} %get-tuple-element.204, ...), kind=kOutput, calls=%fused_computation.30.clone.1 | convolution fusion | flops 172064768 | bytes 608896 | tf_op jit(solution)/shard_map/while/body/eval_jaxpr/vmap(kij,kcj->ci)/dot_general | solution.py:30
  153.3 12.0 %fusion.64 = f32[4,6,128]{2,1,0:T(8,128)S(1)} fusion(f32[4,32,128]{2,1,0:T(8,128)S(1)} %bitcast.126, f32[4,128]{1,0:T(4,128)S(1)} %get-tuple-element.200, f32[4,32,128]{2,1,0:T(8,128)S(1)} %bitcast.127, f32[4,128]{1,0:T(4,128)S(1)} %get-tuple-element.202, f32[4,32,128]{2,1,0:T(8,128)S(1)} %bitcast.125, f32[4,128]{1,0:T(4,128)S(1)} %get-tuple-element.204, ...), kind=kOutput, calls=%fused_computation.30.clone.1 | convolution fusion | flops 172064768 | bytes 608896 | tf_op jit(solution)/shard_map/while/body/eval_jaxpr/vmap(kij,kcj->ci)/dot_general | solution.py:30
  167.4 12.0 %fusion.64 = f32[4,6,128]{2,1,0:T(8,128)S(1)} fusion(f32[4,32,128]{2,1,0:T(8,128)S(1)} %bitcast.126, f32[4,128]{1,0:T(4,128)S(1)} %get-tuple-element.200, f32[4,32,128]{2,1,0:T(8,128)S(1)} %bitcast.127, f32[4,128]{1,0:T(4,128)S(1)} %get-tuple-element.202, f32[4,32,128]{2,1,0:T(8,128)S(1)} %bitcast.125, f32[4,128]{1,0:T(4,128)S(1)} %get-tuple-element.204, ...), kind=kOutput, calls=%fused_computation.30.clone.1 | convolution fusion | flops 172064768 | bytes 608896 | tf_op jit(solution)/shard_map/while/body/eval_jaxpr/vmap(kij,kcj->ci)/dot_general | solution.py:30
  181.6 12.0 %fusion.64 = f32[4,6,128]{2,1,0:T(8,128)S(1)} fusion(f32[4,32,128]{2,1,0:T(8,128)S(1)} %bitcast.126, f32[4,128]{1,0:T(4,128)S(1)} %get-tuple-element.200, f32[4,32,128]{2,1,0:T(8,128)S(1)} %bitcast.127, f32[4,128]{1,0:T(4,128)S(1)} %get-tuple-element.202, f32[4,32,128]{2,1,0:T(8,128)S(1)} %bitcast.125, f32[4,128]{1,0:T(4,128)S(1)} %get-tuple-element.204, ...), kind=kOutput, calls=%fused_computation.30.clone.1 | convolution fusion | flops 172064768 | bytes 608896 | tf_op jit(solution)/shard_map/while/body/eval_jaxpr/vmap(kij,kcj->ci)/dot_general | solution.py:30
  195.8 12.0 %fusion.64 = f32[4,6,128]{2,1,0:T(8,128)S(1)} fusion(f32[4,32,128]{2,1,0:T(8,128)S(1)} %bitcast.126, f32[4,128]{1,0:T(4,128)S(1)} %get-tuple-element.200, f32[4,32,128]{2,1,0:T(8,128)S(1)} %bitcast.127, f32[4,128]{1,0:T(4,128)S(1)} %get-tuple-element.202, f32[4,32,128]{2,1,0:T(8,128)S(1)} %bitcast.125, f32[4,128]{1,0:T(4,128)S(1)} %get-tuple-element.204, ...), kind=kOutput, calls=%fused_computation.30.clone.1 | convolution fusion | flops 172064768 | bytes 608896 | tf_op jit(solution)/shard_map/while/body/eval_jaxpr/vmap(kij,kcj->ci)/dot_general | solution.py:30
  209.9 12.0 %fusion.64 = f32[4,6,128]{2,1,0:T(8,128)S(1)} fusion(f32[4,32,128]{2,1,0:T(8,128)S(1)} %bitcast.126, f32[4,128]{1,0:T(4,128)S(1)} %get-tuple-element.200, f32[4,32,128]{2,1,0:T(8,128)S(1)} %bitcast.127, f32[4,128]{1,0:T(4,128)S(1)} %get-tuple-element.202, f32[4,32,128]{2,1,0:T(8,128)S(1)} %bitcast.125, f32[4,128]{1,0:T(4,128)S(1)} %get-tuple-element.204, ...), kind=kOutput, calls=%fused_computation.30.clone.1 | convolution fusion | flops 172064768 | bytes 608896 | tf_op jit(solution)/shard_map/while/body/eval_jaxpr/vmap(kij,kcj->ci)/dot_general | solution.py:30
  224.1 12.0 %fusion.64 = f32[4,6,128]{2,1,0:T(8,128)S(1)} fusion(f32[4,32,128]{2,1,0:T(8,128)S(1)} %bitcast.126, f32[4,128]{1,0:T(4,128)S(1)} %get-tuple-element.200, f32[4,32,128]{2,1,0:T(8,128)S(1)} %bitcast.127, f32[4,128]{1,0:T(4,128)S(1)} %get-tuple-element.202, f32[4,32,128]{2,1,0:T(8,128)S(1)} %bitcast.125, f32[4,128]{1,0:T(4,128)S(1)} %get-tuple-element.204, ...), kind=kOutput, calls=%fused_computation.30.clone.1 | convolution fusion | flops 172064768 | bytes 608896 | tf_op jit(solution)/shard_map/while/body/eval_jaxpr/vmap(kij,kcj->ci)/dot_general | solution.py:30
  238.3 12.0 %fusion.64 = f32[4,6,128]{2,1,0:T(8,128)S(1)} fusion(f32[4,32,128]{2,1,0:T(8,128)S(1)} %bitcast.126, f32[4,128]{1,0:T(4,128)S(1)} %get-tuple-element.200, f32[4,32,128]{2,1,0:T(8,128)S(1)} %bitcast.127, f32[4,128]{1,0:T(4,128)S(1)} %get-tuple-element.202, f32[4,32,128]{2,1,0:T(8,128)S(1)} %bitcast.125, f32[4,128]{1,0:T(4,128)S(1)} %get-tuple-element.204, ...), kind=kOutput, calls=%fused_computation.30.clone.1 | convolution fusion | flops 172064768 | bytes 608896 | tf_op jit(solution)/shard_map/while/body/eval_jaxpr/vmap(kij,kcj->ci)/dot_general | solution.py:30
  252.4 12.0 %fusion.64 = f32[4,6,128]{2,1,0:T(8,128)S(1)} fusion(f32[4,32,128]{2,1,0:T(8,128)S(1)} %bitcast.126, f32[4,128]{1,0:T(4,128)S(1)} %get-tuple-element.200, f32[4,32,128]{2,1,0:T(8,128)S(1)} %bitcast.127, f32[4,128]{1,0:T(4,128)S(1)} %get-tuple-element.202, f32[4,32,128]{2,1,0:T(8,128)S(1)} %bitcast.125, f32[4,128]{1,0:T(4,128)S(1)} %get-tuple-element.204, ...), kind=kOutput, calls=%fused_computation.30.clone.1 | convolution fusion | flops 172064768 | bytes 608896 | tf_op jit(solution)/shard_map/while/body/eval_jaxpr/vmap(kij,kcj->ci)/dot_general | solution.py:30
  266.6 12.0 %fusion.64 = f32[4,6,128]{2,1,0:T(8,128)S(1)} fusion(f32[4,32,128]{2,1,0:T(8,128)S(1)} %bitcast.126, f32[4,128]{1,0:T(4,128)S(1)} %get-tuple-element.200, f32[4,32,128]{2,1,0:T(8,128)S(1)} %bitcast.127, f32[4,128]{1,0:T(4,128)S(1)} %get-tuple-element.202, f32[4,32,128]{2,1,0:T(8,128)S(1)} %bitcast.125, f32[4,128]{1,0:T(4,128)S(1)} %get-tuple-element.204, ...), kind=kOutput, calls=%fused_computation.30.clone.1 | convolution fusion | flops 172064768 | bytes 608896 | tf_op jit(solution)/shard_map/while/body/eval_jaxpr/vmap(kij,kcj->ci)/dot_general | solution.py:30
  280.7 12.0 %fusion.64 = f32[4,6,128]{2,1,0:T(8,128)S(1)} fusion(f32[4,32,128]{2,1,0:T(8,128)S(1)} %bitcast.126, f32[4,128]{1,0:T(4,128)S(1)} %get-tuple-element.200, f32[4,32,128]{2,1,0:T(8,128)S(1)} %bitcast.127, f32[4,128]{1,0:T(4,128)S(1)} %get-tuple-element.202, f32[4,32,128]{2,1,0:T(8,128)S(1)} %bitcast.125, f32[4,128]{1,0:T(4,128)S(1)} %get-tuple-element.204, ...), kind=kOutput, calls=%fused_computation.30.clone.1 | convolution fusion | flops 172064768 | bytes 608896 | tf_op jit(solution)/shard_map/while/body/eval_jaxpr/vmap(kij,kcj->ci)/dot_general | solution.py:30
  294.9 12.0 %fusion.64 = f32[4,6,128]{2,1,0:T(8,128)S(1)} fusion(f32[4,32,128]{2,1,0:T(8,128)S(1)} %bitcast.126, f32[4,128]{1,0:T(4,128)S(1)} %get-tuple-element.200, f32[4,32,128]{2,1,0:T(8,128)S(1)} %bitcast.127, f32[4,128]{1,0:T(4,128)S(1)} %get-tuple-element.202, f32[4,32,128]{2,1,0:T(8,128)S(1)} %bitcast.125, f32[4,128]{1,0:T(4,128)S(1)} %get-tuple-element.204, ...), kind=kOutput, calls=%fused_computation.30.clone.1 | convolution fusion | flops 172064768 | bytes 608896 | tf_op jit(solution)/shard_map/while/body/eval_jaxpr/vmap(kij,kcj->ci)/dot_general | solution.py:30
  307.9 6.6 %scatter_fusion.2 = f32[128,3,128]{2,1,0:T(4,128)} fusion(f32[128,3,128]{2,1,0:T(4,128)} %broadcast_in_dim.90, s32[64]{0:T(128)S(1)} %compare_select_fusion.4, f32[64,3,128]{2,1,0:T(4,128)S(1)} %copy.114), kind=kCustom, calls=%fused_computation.7 | custom fusion | bytes 295168 | tf_op jit(solution)/shard_map/scatter | solution.py:44
  314.5 6.0 %all-to-all-start.3 = ((f32[128,3,128]{2,1,0:T(4,128)}), f32[128,3,128]{2,1,0:T(4,128)S(1)}, u32[]{:S(2)}, u32[]{:S(2)}) async-start(f32[128,3,128]{2,1,0:T(4,128)} %scatter_fusion.2), calls=%async_computation.3 | async-start | bytes 524288 | tf_op jit(solution)/shard_map/all_to_all | solution.py:114
  321.6 0.8 copy.115
  322.5 8.1 %all-to-all-done.3 = f32[128,3,128]{2,1,0:T(4,128)S(1)} async-done(((f32[128,3,128]{2,1,0:T(4,128)}), f32[128,3,128]{2,1,0:T(4,128)S(1)}, u32[]{:S(2)}, u32[]{:S(2)}) %all-to-all-start.3) | async-done | bytes 196640 | tf_op jit(solution)/shard_map/all_to_all | solution.py:114
  330.6 4.5 %scatter_fusion.3 = f32[64,3,128]{2,1,0:T(4,128)S(1)} fusion(f32[64,3,128]{2,1,0:T(4,128)S(1)} %broadcast_in_dim.88, s32[128]{0:T(128)S(1)} %fusion.46, f32[128,3,128]{2,1,0:T(4,128)S(1)} %all-to-all-done.3), kind=kCustom, calls=%fused_computation.8 | custom fusion | bytes 590336 | tf_op jit(solution)/shard_map/scatter | solution.py:57
  (297 shorter events, 47.7 us)
Async XLA Ops:
  7.2 63.5 %all-gather.2.cloned.1.call-start = ((), (), s32[]{:S(2)}) async-start(), calls=%async_computation.4 | async-start | bytes 3342336 | tf_op jit(solution)/shard_map/all_gather | solution.py:79
  11.4 23.3 %all-to-all-start = ((f32[16,8,1]{1,2,0:T(1,128)}), f32[16,8,1]{1,2,0:T(1,128)S(1)}, u32[]{:S(2)}, u32[]{:S(2)}) async-start(f32[16,8,1]{1,2,0:T(1,128)} %bitcast.25), calls=%async_computation | async-start | bytes 16384 | tf_op jit(solution)/shard_map/all_to_all | solution.py:105
  34.7 24.8 %all-to-all-start.1 = ((f32[128,2,3,128]{3,1,2,0:T(2,128)}), f32[128,2,3,128]{3,1,2,0:T(2,128)S(1)}, u32[]{:S(2)}, u32[]{:S(2)}) async-start(f32[128,2,3,128]{3,1,2,0:T(2,128)} %scatter_fusion), calls=%async_computation.1 | async-start | bytes 786432 | tf_op jit(solution)/shard_map/all_to_all | solution.py:104
  59.5 255.0 %all-to-all-start.2 = ((f32[16,8,1]{1,2,0:T(1,128)}), f32[16,8,1]{1,2,0:T(1,128)S(1)}, u32[]{:S(2)}, u32[]{:S(2)}) async-start(f32[16,8,1]{1,2,0:T(1,128)} %bitcast.31), calls=%async_computation.2 | async-start | bytes 16384 | tf_op jit(solution)/shard_map/all_to_all | solution.py:115
  76.4 3.8 %copy-start = (f32[64,3,128]{2,0,1:T(8,128)S(1)}, f32[64,3,128]{2,0,1:T(8,128)}, u32[]{:S(2)}) copy-start(f32[64,3,128]{2,0,1:T(8,128)} %param.13) | copy-start | bytes 294916
  80.2 240.3 %copy-start.2 = (s32[64,128]{1,0:T(8,128)S(1)}, s32[64,128]{1,0:T(8,128)}, u32[]{:S(2)}) copy-start(s32[64,128]{1,0:T(8,128)} %param.21) | copy-start | bytes 98308
  307.1 28.9 %copy-start.1 = (f32[64,3,128]{2,0,1:T(8,128)}, f32[64,3,128]{2,0,1:T(8,128)S(1)}, u32[]{:S(2)}) copy-start(f32[64,3,128]{2,0,1:T(8,128)S(1)} %fusion.36) | copy-start | bytes 294916
  314.5 16.0 %all-to-all-start.3 = ((f32[128,3,128]{2,1,0:T(4,128)}), f32[128,3,128]{2,1,0:T(4,128)S(1)}, u32[]{:S(2)}, u32[]{:S(2)}) async-start(f32[128,3,128]{2,1,0:T(4,128)} %scatter_fusion.2), calls=%async_computation.3 | async-start | bytes 524288 | tf_op jit(solution)/shard_map/all_to_all | solution.py:114
Sparse Core Ops, SparseCore 0:
  10.8 54.3 all-gather.1
where the time goes:
time: 344 us; the launch traced here: 343 us
  matrix products  192 us (56%)
  local copies, waits for them, and re-layouts  70.9 us (21%)
  starting transfers between devices  25.7 us (7%)
  waiting for transfers between devices  25.5 us (7%)
  between operations  14.4 us (4%)
  other arithmetic  12.3 us (4%)
    dot_general x16, matrix products, induced(): jnp.einsum('kij,kcj->ci', weight, source_table, precision=lax.Precision.H...  192 us
    all_to_all x1, waiting for transfers between devices, body(): lax.all_to_all(buffer, 'box', split_axis=0, concat_axis=0, tiled=True)  17.4 us
    scatter x2, local copies, waits for them, and re-layouts, pack_blocks(): jnp.zeros((box_count * capacity,) + values.shape[1:], values.dtype)  14.5 us
    gather x16, local copies, waits for them, and re-layouts, one_target(): jnp.take(source_table, slots, axis=0)  12.2 us
    gather x16, local copies, waits for them, and re-layouts, one_target(): jnp.take(source_pos, slots, axis=0)  12 us
    scatter x2, local copies, waits for them, and re-layouts, unpack_blocks(): jnp.zeros((blocks,) + arrived.shape[1:], arrived.dtype).at[place]  9.19 us
    all_to_all x1, waiting for transfers between devices, body(): lax.all_to_all(age_buffer, 'box', split_axis=0, concat_axis=0, tiled=True)  8.07 us
    all_to_all x1, starting transfers between devices, body(): lax.all_to_all(labels, 'box', split_axis=0, concat_axis=0, tiled=True)  7.39 us
  transfers between devices with their start and end apart: 5, of which 2 were waited for; matrix products, arithmetic and copies ran while one was open for 78% of the time, Pallas kernels for 0%

commit v1 on v0

--- a/solution.py
+++ b/solution.py
@@ -8,6 +8,29 @@
 BLADES = 3
 core_square = 0.05
 time_step = 0.05
+
+
+def in_blocks(x, dim, peers):
+    dims = x.shape
+    blocks = x.reshape(*dims[:dim], peers, dims[dim] // peers, *dims[dim + 1 :])
+    return jnp.moveaxis(blocks, dim, 0)
+
+
+def in_order(parts, dim):
+    parts = jnp.moveaxis(parts, 0, dim)
+    shape = parts.shape
+    return parts.reshape(*shape[:dim], shape[dim] * shape[dim + 1], *shape[dim + 2 :])
+
+
+def sent_to_each(array, axis, split_dim, concat_dim):
+    length, position = (lax.axis_size(axis), lax.axis_index(axis))
+    blocks = in_blocks(array, split_dim, length)
+    outs = [blocks[position]]
+    for step in range(1, length):
+        sent = blocks[(position + step) % length]
+        outs.append(lax.ppermute(sent, axis, [(i, (i + step) % length) for i in range(length)]))
+    blocks = jnp.stack(outs)[(position - jnp.arange(length)) % length]
+    return in_order(blocks, concat_dim)
 
 
 def cross_product(first, second):
@@ -111,7 +134,7 @@
     new_history = jnp.stack([velocity, moved[:, 0]], axis=1)
     age_buffer, age_labels = pack_blocks(new_positions, age_slot, blocks, box_count, capacity)
     aged_in, aged_labels = (
-        lax.all_to_all(age_buffer, "box", split_axis=0, concat_axis=0, tiled=True),
+        sent_to_each(age_buffer, "box", 0, 0),
         lax.all_to_all(age_labels, "box", split_axis=0, concat_axis=0, tiled=True),
     )
     aged = unpack_blocks(aged_in, aged_labels, blocks)

time: 344 us -> 347 us (level)
  starting transfers between devices: 25.7 us -> 40.1 us
  waiting for transfers between devices: 25.5 us -> 16.6 us
  local copies, waits for them, and re-layouts: 70.9 us -> 67.1 us
    ppermute x0 -> x15, starting transfers between devices: none -> 20.9 us  [sent_to_each(): lax.ppermute(sent, axis, [(i, (i + step) % length) for i in range(length)])]
    all_to_all x1 -> x0, waiting for transfers between devices: 8.07 us -> none  [body(): lax.all_to_all(age_buffer, 'box', split_axis=0, concat_axis=0, tiled=True)]
    all_to_all x1 -> x0, starting transfers between devices: 5.99 us -> none  [body(): lax.all_to_all(age_buffer, 'box', split_axis=0, concat_axis=0, tiled=True)]
    scatter x2 -> x3, local copies, waits for them, and re-layouts: 14.5 us -> 10.6 us  [pack_blocks(): jnp.zeros((box_count * capacity,) + values.shape[1:], values.dtype)]
  transfers between devices with their start and end apart: 5 -> 19, of which waited for: 2 -> 3; matrix products, arithmetic and copies ran while one was open for 78% -> 7% of each run, Pallas kernels for 0% -> 0%
where the time goes in v1:
time: 347 us; the launch traced here: 346 us
  matrix products  192 us (55%)
  local copies, waits for them, and re-layouts  67.1 us (19%)
  starting transfers between devices  40.1 us (12%)
  waiting for transfers between devices  16.6 us (5%)
  between operations  14.8 us (4%)
  other arithmetic  13.1 us (4%)
    dot_general x16, matrix products, induced(): jnp.einsum('kij,kcj->ci', weight, source_table, precision=lax.Precision.H...  192 us
    ppermute x15, starting transfers between devices, sent_to_each(): lax.ppermute(sent, axis, [(i, (i + step) % length) for i in range(length)])  20.9 us
    all_to_all x1, waiting for transfers between devices, body(): lax.all_to_all(buffer, 'box', split_axis=0, concat_axis=0, tiled=True)  14.3 us
    gather x16, local copies, waits for them, and re-layouts, one_target(): jnp.take(source_table, slots, axis=0)  12.2 us
    gather x16, local copies, waits for them, and re-layouts, one_target(): jnp.take(source_pos, slots, axis=0)  12 us
    scatter x3, local copies, waits for them, and re-layouts, pack_blocks(): jnp.zeros((box_count * capacity,) + values.shape[1:], values.dtype)  10.6 us
    scatter x2, local copies, waits for them, and re-layouts, unpack_blocks(): jnp.zeros((blocks,) + arrived.shape[1:], arrived.dtype).at[place]  9.19 us
    all_to_all x1, starting transfers between devices, body(): lax.all_to_all(labels, 'box', split_axis=0, concat_axis=0, tiled=True)  7.39 us
  transfers between devices with their start and end apart: 19, of which 3 were waited for; matrix products, arithmetic and copies ran while one was open for 7% of the time, Pallas kernels for 0%

profile of v1, /device:TPU:0, one launch (start us, length us, event | category | flops | bytes accessed | tf_op | source)
XLA Modules:
  0.0 345.7 jit_solution(16363712468963476601)
XLA Ops:
  12.4 7.4 %all-to-all-start = ((f32[16,8,1]{1,2,0:T(1,128)}), f32[16,8,1]{1,2,0:T(1,128)S(1)}, u32[]{:S(2)}, u32[]{:S(2)}) async-start(f32[16,8,1]{1,2,0:T(1,128)} %bitcast.25), calls=%async_computation | async-start | bytes 16384 | tf_op jit(solution)/shard_map/all_to_all | solution.py:128
  27.1 5.8 %all-to-all-start.2 = ((f32[16,8,1]{1,2,0:T(1,128)}), f32[16,8,1]{1,2,0:T(1,128)S(1)}, u32[]{:S(2)}, u32[]{:S(2)}) async-start(f32[16,8,1]{1,2,0:T(1,128)} %bitcast.31), calls=%async_computation.2 | async-start | bytes 16384 | tf_op jit(solution)/shard_map/all_to_all | solution.py:138
  33.9 8.0 %scatter_fusion = f32[128,2,3,128]{3,1,2,0:T(2,128)} fusion(f32[128,2,3,128]{3,1,2,0:T(2,128)} %broadcast_in_dim.88, s32[64]{0:T(128)S(1)} %get-tuple-element.170, f32[64,2,3,128]{3,1,2,0:T(2,128)} %param.15), kind=kCustom, calls=%fused_computation.5 | custom fusion | bytes 590080 | tf_op jit(solution)/shard_map/scatter | solution.py:67
  41.9 6.0 %all-to-all-start.1 = ((f32[128,2,3,128]{3,1,2,0:T(2,128)}), f32[128,2,3,128]{3,1,2,0:T(2,128)S(1)}, u32[]{:S(2)}, u32[]{:S(2)}) async-start(f32[128,2,3,128]{3,1,2,0:T(2,128)} %scatter_fusion), calls=%async_computation.1 | async-start | bytes 786432 | tf_op jit(solution)/shard_map/all_to_all | solution.py:127
  50.0 14.3 %all-to-all-done.1 = f32[128,2,3,128]{3,1,2,0:T(2,128)S(1)} async-done(((f32[128,2,3,128]{3,1,2,0:T(2,128)}), f32[128,2,3,128]{3,1,2,0:T(2,128)S(1)}, u32[]{:S(2)}, u32[]{:S(2)}) %all-to-all-start.1) | async-done | bytes 393248 | tf_op jit(solution)/shard_map/all_to_all | solution.py:127
  64.3 4.7 %scatter_fusion.1 = f32[64,2,3,128]{3,1,2,0:T(2,128)S(1)} fusion(f32[64,2,3,128]{3,1,2,0:T(2,128)S(1)} %broadcast_in_dim.85, s32[128]{0:T(128)S(1)} %fusion.45, f32[128,2,3,128]{3,1,2,0:T(2,128)S(1)} %all-to-all-done.1), kind=kCustom, calls=%fused_computation.6 | custom fusion | bytes 1180160 | tf_op jit(solution)/shard_map/scatter | solution.py:80
  69.2 5.7 %copy.138 = f32[1024,6,128]{2,1,0:T(8,128)} copy(f32[1024,6,128]{2,0,1:T(8,128)} %all-gather.2.cloned.1.call-done) | data formatting | bytes 6291456 | tf_op jit(solution)/shard_map/all_gather | solution.py:102
  75.0 2.9 gather_fusion.2
  78.7 226.8 %while.10 = (s32[]{:T(128)}, f32[16,4,3,128]{3,2,1,0:T(4,128)S(1)}, f32[16,4,3,128]{3,1,0,2:T(4,128)S(1)}, s32[16,4,32]{2,1,0:T(4,128)S(1)}, f32[128,6,128]{2,1,...) while((s32[]{:T(128)}, f32[16,4,3,128]{3,2,1,0:T(4,128)S(1)}, ...), condition=%wide.region_1.2_spmd, body=%wide.region_0.1_spmd.sunk | while | flops 172126848 | bytes 2662377 | solution.py:124
  81.0 12.0 %fusion.66 = f32[4,6,128]{2,1,0:T(8,128)S(1)} fusion(f32[4,32,128]{2,1,0:T(8,128)S(1)} %bitcast.196, f32[4,128]{1,0:T(4,128)S(1)} %get-tuple-element.227, f32[4,32,128]{2,1,0:T(8,128)S(1)} %bitcast.197, f32[4,128]{1,0:T(4,128)S(1)} %get-tuple-element.229, f32[4,32,128]{2,1,0:T(8,128)S(1)} %bitcast.195, f32[4,128]{1,0:T(4,128)S(1)} %get-tuple-element.231, ...), kind=kOutput, calls=%fused_computation.31.clone.1 | convolution fusion | flops 172064768 | bytes 608896 | tf_op jit(solution)/shard_map/while/body/eval_jaxpr/vmap(kij,kcj->ci)/dot_general | solution.py:53
  95.2 12.0 %fusion.66 = f32[4,6,128]{2,1,0:T(8,128)S(1)} fusion(f32[4,32,128]{2,1,0:T(8,128)S(1)} %bitcast.196, f32[4,128]{1,0:T(4,128)S(1)} %get-tuple-element.227, f32[4,32,128]{2,1,0:T(8,128)S(1)} %bitcast.197, f32[4,128]{1,0:T(4,128)S(1)} %get-tuple-element.229, f32[4,32,128]{2,1,0:T(8,128)S(1)} %bitcast.195, f32[4,128]{1,0:T(4,128)S(1)} %get-tuple-element.231, ...), kind=kOutput, calls=%fused_computation.31.clone.1 | convolution fusion | flops 172064768 | bytes 608896 | tf_op jit(solution)/shard_map/while/body/eval_jaxpr/vmap(kij,kcj->ci)/dot_general | solution.py:53
  109.3 12.0 %fusion.66 = f32[4,6,128]{2,1,0:T(8,128)S(1)} fusion(f32[4,32,128]{2,1,0:T(8,128)S(1)} %bitcast.196, f32[4,128]{1,0:T(4,128)S(1)} %get-tuple-element.227, f32[4,32,128]{2,1,0:T(8,128)S(1)} %bitcast.197, f32[4,128]{1,0:T(4,128)S(1)} %get-tuple-element.229, f32[4,32,128]{2,1,0:T(8,128)S(1)} %bitcast.195, f32[4,128]{1,0:T(4,128)S(1)} %get-tuple-element.231, ...), kind=kOutput, calls=%fused_computation.31.clone.1 | convolution fusion | flops 172064768 | bytes 608896 | tf_op jit(solution)/shard_map/while/body/eval_jaxpr/vmap(kij,kcj->ci)/dot_general | solution.py:53
  123.5 12.0 %fusion.66 = f32[4,6,128]{2,1,0:T(8,128)S(1)} fusion(f32[4,32,128]{2,1,0:T(8,128)S(1)} %bitcast.196, f32[4,128]{1,0:T(4,128)S(1)} %get-tuple-element.227, f32[4,32,128]{2,1,0:T(8,128)S(1)} %bitcast.197, f32[4,128]{1,0:T(4,128)S(1)} %get-tuple-element.229, f32[4,32,128]{2,1,0:T(8,128)S(1)} %bitcast.195, f32[4,128]{1,0:T(4,128)S(1)} %get-tuple-element.231, ...), kind=kOutput, calls=%fused_computation.31.clone.1 | convolution fusion | flops 172064768 | bytes 608896 | tf_op jit(solution)/shard_map/while/body/eval_jaxpr/vmap(kij,kcj->ci)/dot_general | solution.py:53
  137.7 12.0 %fusion.66 = f32[4,6,128]{2,1,0:T(8,128)S(1)} fusion(f32[4,32,128]{2,1,0:T(8,128)S(1)} %bitcast.196, f32[4,128]{1,0:T(4,128)S(1)} %get-tuple-element.227, f32[4,32,128]{2,1,0:T(8,128)S(1)} %bitcast.197, f32[4,128]{1,0:T(4,128)S(1)} %get-tuple-element.229, f32[4,32,128]{2,1,0:T(8,128)S(1)} %bitcast.195, f32[4,128]{1,0:T(4,128)S(1)} %get-tuple-element.231, ...), kind=kOutput, calls=%fused_computation.31.clone.1 | convolution fusion | flops 172064768 | bytes 608896 | tf_op jit(solution)/shard_map/while/body/eval_jaxpr/vmap(kij,kcj->ci)/dot_general | solution.py:53
  151.8 12.0 %fusion.66 = f32[4,6,128]{2,1,0:T(8,128)S(1)} fusion(f32[4,32,128]{2,1,0:T(8,128)S(1)} %bitcast.196, f32[4,128]{1,0:T(4,128)S(1)} %get-tuple-element.227, f32[4,32,128]{2,1,0:T(8,128)S(1)} %bitcast.197, f32[4,128]{1,0:T(4,128)S(1)} %get-tuple-element.229, f32[4,32,128]{2,1,0:T(8,128)S(1)} %bitcast.195, f32[4,128]{1,0:T(4,128)S(1)} %get-tuple-element.231, ...), kind=kOutput, calls=%fused_computation.31.clone.1 | convolution fusion | flops 172064768 | bytes 608896 | tf_op jit(solution)/shard_map/while/body/eval_jaxpr/vmap(kij,kcj->ci)/dot_general | solution.py:53
  166.0 12.0 %fusion.66 = f32[4,6,128]{2,1,0:T(8,128)S(1)} fusion(f32[4,32,128]{2,1,0:T(8,128)S(1)} %bitcast.196, f32[4,128]{1,0:T(4,128)S(1)} %get-tuple-element.227, f32[4,32,128]{2,1,0:T(8,128)S(1)} %bitcast.197, f32[4,128]{1,0:T(4,128)S(1)} %get-tuple-element.229, f32[4,32,128]{2,1,0:T(8,128)S(1)} %bitcast.195, f32[4,128]{1,0:T(4,128)S(1)} %get-tuple-element.231, ...), kind=kOutput, calls=%fused_computation.31.clone.1 | convolution fusion | flops 172064768 | bytes 608896 | tf_op jit(solution)/shard_map/while/body/eval_jaxpr/vmap(kij,kcj->ci)/dot_general | solution.py:53
  180.1 12.0 %fusion.66 = f32[4,6,128]{2,1,0:T(8,128)S(1)} fusion(f32[4,32,128]{2,1,0:T(8,128)S(1)} %bitcast.196, f32[4,128]{1,0:T(4,128)S(1)} %get-tuple-element.227, f32[4,32,128]{2,1,0:T(8,128)S(1)} %bitcast.197, f32[4,128]{1,0:T(4,128)S(1)} %get-tuple-element.229, f32[4,32,128]{2,1,0:T(8,128)S(1)} %bitcast.195, f32[4,128]{1,0:T(4,128)S(1)} %get-tuple-element.231, ...), kind=kOutput, calls=%fused_computation.31.clone.1 | convolution fusion | flops 172064768 | bytes 608896 | tf_op jit(solution)/shard_map/while/body/eval_jaxpr/vmap(kij,kcj->ci)/dot_general | solution.py:53
  194.3 12.0 %fusion.66 = f32[4,6,128]{2,1,0:T(8,128)S(1)} fusion(f32[4,32,128]{2,1,0:T(8,128)S(1)} %bitcast.196, f32[4,128]{1,0:T(4,128)S(1)} %get-tuple-element.227, f32[4,32,128]{2,1,0:T(8,128)S(1)} %bitcast.197, f32[4,128]{1,0:T(4,128)S(1)} %get-tuple-element.229, f32[4,32,128]{2,1,0:T(8,128)S(1)} %bitcast.195, f32[4,128]{1,0:T(4,128)S(1)} %get-tuple-element.231, ...), kind=kOutput, calls=%fused_computation.31.clone.1 | convolution fusion | flops 172064768 | bytes 608896 | tf_op jit(solution)/shard_map/while/body/eval_jaxpr/vmap(kij,kcj->ci)/dot_general | solution.py:53
  208.5 12.0 %fusion.66 = f32[4,6,128]{2,1,0:T(8,128)S(1)} fusion(f32[4,32,128]{2,1,0:T(8,128)S(1)} %bitcast.196, f32[4,128]{1,0:T(4,128)S(1)} %get-tuple-element.227, f32[4,32,128]{2,1,0:T(8,128)S(1)} %bitcast.197, f32[4,128]{1,0:T(4,128)S(1)} %get-tuple-element.229, f32[4,32,128]{2,1,0:T(8,128)S(1)} %bitcast.195, f32[4,128]{1,0:T(4,128)S(1)} %get-tuple-element.231, ...), kind=kOutput, calls=%fused_computation.31.clone.1 | convolution fusion | flops 172064768 | bytes 608896 | tf_op jit(solution)/shard_map/while/body/eval_jaxpr/vmap(kij,kcj->ci)/dot_general | solution.py:53
  222.6 12.0 %fusion.66 = f32[4,6,128]{2,1,0:T(8,128)S(1)} fusion(f32[4,32,128]{2,1,0:T(8,128)S(1)} %bitcast.196, f32[4,128]{1,0:T(4,128)S(1)} %get-tuple-element.227, f32[4,32,128]{2,1,0:T(8,128)S(1)} %bitcast.197, f32[4,128]{1,0:T(4,128)S(1)} %get-tuple-element.229, f32[4,32,128]{2,1,0:T(8,128)S(1)} %bitcast.195, f32[4,128]{1,0:T(4,128)S(1)} %get-tuple-element.231, ...), kind=kOutput, calls=%fused_computation.31.clone.1 | convolution fusion | flops 172064768 | bytes 608896 | tf_op jit(solution)/shard_map/while/body/eval_jaxpr/vmap(kij,kcj->ci)/dot_general | solution.py:53
  236.8 12.0 %fusion.66 = f32[4,6,128]{2,1,0:T(8,128)S(1)} fusion(f32[4,32,128]{2,1,0:T(8,128)S(1)} %bitcast.196, f32[4,128]{1,0:T(4,128)S(1)} %get-tuple-element.227, f32[4,32,128]{2,1,0:T(8,128)S(1)} %bitcast.197, f32[4,128]{1,0:T(4,128)S(1)} %get-tuple-element.229, f32[4,32,128]{2,1,0:T(8,128)S(1)} %bitcast.195, f32[4,128]{1,0:T(4,128)S(1)} %get-tuple-element.231, ...), kind=kOutput, calls=%fused_computation.31.clone.1 | convolution fusion | flops 172064768 | bytes 608896 | tf_op jit(solution)/shard_map/while/body/eval_jaxpr/vmap(kij,kcj->ci)/dot_general | solution.py:53
  251.0 12.0 %fusion.66 = f32[4,6,128]{2,1,0:T(8,128)S(1)} fusion(f32[4,32,128]{2,1,0:T(8,128)S(1)} %bitcast.196, f32[4,128]{1,0:T(4,128)S(1)} %get-tuple-element.227, f32[4,32,128]{2,1,0:T(8,128)S(1)} %bitcast.197, f32[4,128]{1,0:T(4,128)S(1)} %get-tuple-element.229, f32[4,32,128]{2,1,0:T(8,128)S(1)} %bitcast.195, f32[4,128]{1,0:T(4,128)S(1)} %get-tuple-element.231, ...), kind=kOutput, calls=%fused_computation.31.clone.1 | convolution fusion | flops 172064768 | bytes 608896 | tf_op jit(solution)/shard_map/while/body/eval_jaxpr/vmap(kij,kcj->ci)/dot_general | solution.py:53
  265.1 12.0 %fusion.66 = f32[4,6,128]{2,1,0:T(8,128)S(1)} fusion(f32[4,32,128]{2,1,0:T(8,128)S(1)} %bitcast.196, f32[4,128]{1,0:T(4,128)S(1)} %get-tuple-element.227, f32[4,32,128]{2,1,0:T(8,128)S(1)} %bitcast.197, f32[4,128]{1,0:T(4,128)S(1)} %get-tuple-element.229, f32[4,32,128]{2,1,0:T(8,128)S(1)} %bitcast.195, f32[4,128]{1,0:T(4,128)S(1)} %get-tuple-element.231, ...), kind=kOutput, calls=%fused_computation.31.clone.1 | convolution fusion | flops 172064768 | bytes 608896 | tf_op jit(solution)/shard_map/while/body/eval_jaxpr/vmap(kij,kcj->ci)/dot_general | solution.py:53
  279.3 12.0 %fusion.66 = f32[4,6,128]{2,1,0:T(8,128)S(1)} fusion(f32[4,32,128]{2,1,0:T(8,128)S(1)} %bitcast.196, f32[4,128]{1,0:T(4,128)S(1)} %get-tuple-element.227, f32[4,32,128]{2,1,0:T(8,128)S(1)} %bitcast.197, f32[4,128]{1,0:T(4,128)S(1)} %get-tuple-element.229, f32[4,32,128]{2,1,0:T(8,128)S(1)} %bitcast.195, f32[4,128]{1,0:T(4,128)S(1)} %get-tuple-element.231, ...), kind=kOutput, calls=%fused_computation.31.clone.1 | convolution fusion | flops 172064768 | bytes 608896 | tf_op jit(solution)/shard_map/while/body/eval_jaxpr/vmap(kij,kcj->ci)/dot_general | solution.py:53
  293.5 12.0 %fusion.66 = f32[4,6,128]{2,1,0:T(8,128)S(1)} fusion(f32[4,32,128]{2,1,0:T(8,128)S(1)} %bitcast.196, f32[4,128]{1,0:T(4,128)S(1)} %get-tuple-element.227, f32[4,32,128]{2,1,0:T(8,128)S(1)} %bitcast.197, f32[4,128]{1,0:T(4,128)S(1)} %get-tuple-element.229, f32[4,32,128]{2,1,0:T(8,128)S(1)} %bitcast.195, f32[4,128]{1,0:T(4,128)S(1)} %get-tuple-element.231, ...), kind=kOutput, calls=%fused_computation.31.clone.1 | convolution fusion | flops 172064768 | bytes 608896 | tf_op jit(solution)/shard_map/while/body/eval_jaxpr/vmap(kij,kcj->ci)/dot_general | solution.py:53
  305.8 2.7 scatter_fusion.2
  310.3 1.9 collective-permute-start.2
  316.3 2.2 collective-permute-start.6
  318.5 2.0 collective-permute-start.7
  322.4 3.7 %collective-permute-start.10 = (f32[8,3,128]{2,0,1:T(8,128)S(1)}, f32[8,3,128]{2,0,1:T(8,128)S(1)}, u32[]{:S(2)}, u32[]{:S(2)}) collective-permute-start(f32[8,3,128]{2,0,1:T(8,128)S(1)} %get-tuple-element.146), channel_id=1, source_target_pairs={{0,11},{1,12},{2,13},{3,14},{4,15},{5,0},{6,1},{7,2},{8,3},{9,4},{... | collective-permute-start | bytes 36872 | tf_op jit(solution)/shard_map/ppermute | solution.py:31
  328.6 2.6 collective-permute-start.14
  333.5 4.5 %scatter_fusion.3 = f32[64,3,128]{2,1,0:T(4,128)S(1)} fusion(f32[64,3,128]{2,1,0:T(4,128)S(1)} %broadcast_in_dim.89, s32[128]{0:T(128)S(1)} %fusion.47, f32[128,3,128]{2,1,0:T(4,128)S(1)} %copy.150), kind=kCustom, calls=%fused_computation.9 | custom fusion | bytes 590336 | tf_op jit(solution)/shard_map/scatter | solution.py:80
  (345 shorter events, 62.6 us)
Async XLA Ops:
  7.2 62.1 %all-gather.2.cloned.1.call-start = ((), (), s32[]{:S(2)}) async-start(), calls=%async_computation.3 | async-start | bytes 3342336 | tf_op jit(solution)/shard_map/all_gather | solution.py:102
  12.4 14.7 %all-to-all-start = ((f32[16,8,1]{1,2,0:T(1,128)}), f32[16,8,1]{1,2,0:T(1,128)S(1)}, u32[]{:S(2)}, u32[]{:S(2)}) async-start(f32[16,8,1]{1,2,0:T(1,128)} %bitcast.25), calls=%async_computation | async-start | bytes 16384 | tf_op jit(solution)/shard_map/all_to_all | solution.py:128
  27.1 14.7 %all-to-all-start.2 = ((f32[16,8,1]{1,2,0:T(1,128)}), f32[16,8,1]{1,2,0:T(1,128)S(1)}, u32[]{:S(2)}, u32[]{:S(2)}) async-start(f32[16,8,1]{1,2,0:T(1,128)} %bitcast.31), calls=%async_computation.2 | async-start | bytes 16384 | tf_op jit(solution)/shard_map/all_to_all | solution.py:138
  41.9 22.4 %all-to-all-start.1 = ((f32[128,2,3,128]{3,1,2,0:T(2,128)}), f32[128,2,3,128]{3,1,2,0:T(2,128)S(1)}, u32[]{:S(2)}, u32[]{:S(2)}) async-start(f32[128,2,3,128]{3,1,2,0:T(2,128)} %scatter_fusion), calls=%async_computation.1 | async-start | bytes 786432 | tf_op jit(solution)/shard_map/all_to_all | solution.py:127
  75.0 3.8 %copy-start = (f32[64,3,128]{2,0,1:T(8,128)S(1)}, f32[64,3,128]{2,0,1:T(8,128)}, u32[]{:S(2)}) copy-start(f32[64,3,128]{2,0,1:T(8,128)} %param.13) | copy-start | bytes 294916
  305.7 33.2 %copy-start.1 = (f32[64,3,128]{2,0,1:T(8,128)}, f32[64,3,128]{2,0,1:T(8,128)S(1)}, u32[]{:S(2)}) copy-start(f32[64,3,128]{2,0,1:T(8,128)S(1)} %fusion.36) | copy-start | bytes 294916
  308.6 5.9 %collective-permute-start = (f32[8,3,128]{2,0,1:T(8,128)S(1)}, f32[8,3,128]{2,0,1:T(8,128)S(1)}, u32[]{:S(2)}, u32[]{:S(2)}) collective-permute-start(f32[8,3,128]{2,0,1:T(8,128)S(1)} %get-tuple-element.156), channel_id=1, source_target_pairs={{0,1},{1,2},{2,3},{3,4},{4,5},{5,6},{6,7},{7,8},{8,9},{9,10},{10,1... | collective-permute-start | bytes 36872 | tf_op jit(solution)/shard_map/ppermute | solution.py:31
  308.8 7.5 %collective-permute-start.1 = (f32[8,3,128]{2,0,1:T(8,128)S(1)}, f32[8,3,128]{2,0,1:T(8,128)S(1)}, u32[]{:S(2)}, u32[]{:S(2)}) collective-permute-start(f32[8,3,128]{2,0,1:T(8,128)S(1)} %get-tuple-element.155), channel_id=1, source_target_pairs={{0,2},{1,3},{2,4},{3,5},{4,6},{5,7},{6,8},{7,9},{8,10},{9,11},{10,... | collective-permute-start | bytes 36872 | tf_op jit(solution)/shard_map/ppermute | solution.py:31
  310.3 8.2 %collective-permute-start.2 = (f32[8,3,128]{2,0,1:T(8,128)S(1)}, f32[8,3,128]{2,0,1:T(8,128)S(1)}, u32[]{:S(2)}, u32[]{:S(2)}) collective-permute-start(f32[8,3,128]{2,0,1:T(8,128)S(1)} %get-tuple-element.154), channel_id=1, source_target_pairs={{0,3},{1,4},{2,5},{3,6},{4,7},{5,8},{6,9},{7,10},{8,11},{9,12},{10... | collective-permute-start | bytes 36872 | tf_op jit(solution)/shard_map/ppermute | solution.py:31
  312.2 8.3 %collective-permute-start.3 = (f32[8,3,128]{2,0,1:T(8,128)S(1)}, f32[8,3,128]{2,0,1:T(8,128)S(1)}, u32[]{:S(2)}, u32[]{:S(2)}) collective-permute-start(f32[8,3,128]{2,0,1:T(8,128)S(1)} %get-tuple-element.153), channel_id=1, source_target_pairs={{0,4},{1,5},{2,6},{3,7},{4,8},{5,9},{6,10},{7,11},{8,12},{9,13},{1... | collective-permute-start | bytes 36872 | tf_op jit(solution)/shard_map/ppermute | solution.py:31
  312.2 8.3 %collective-permute-start.4 = (f32[8,3,128]{2,0,1:T(8,128)S(1)}, f32[8,3,128]{2,0,1:T(8,128)S(1)}, u32[]{:S(2)}, u32[]{:S(2)}) collective-permute-start(f32[8,3,128]{2,0,1:T(8,128)S(1)} %get-tuple-element.152), channel_id=1, source_target_pairs={{0,5},{1,6},{2,7},{3,8},{4,9},{5,10},{6,11},{7,12},{8,13},{9,14},{... | collective-permute-start | bytes 36872 | tf_op jit(solution)/shard_map/ppermute | solution.py:31
  314.5 7.9 %collective-permute-start.5 = (f32[8,3,128]{2,0,1:T(8,128)S(1)}, f32[8,3,128]{2,0,1:T(8,128)S(1)}, u32[]{:S(2)}, u32[]{:S(2)}) collective-permute-start(f32[8,3,128]{2,0,1:T(8,128)S(1)} %get-tuple-element.151), channel_id=1, source_target_pairs={{0,6},{1,7},{2,8},{3,9},{4,10},{5,11},{6,12},{7,13},{8,14},{9,15},... | collective-permute-start | bytes 36872 | tf_op jit(solution)/shard_map/ppermute | solution.py:31
  316.3 9.8 %collective-permute-start.6 = (f32[8,3,128]{2,0,1:T(8,128)S(1)}, f32[8,3,128]{2,0,1:T(8,128)S(1)}, u32[]{:S(2)}, u32[]{:S(2)}) collective-permute-start(f32[8,3,128]{2,0,1:T(8,128)S(1)} %get-tuple-element.150), channel_id=1, source_target_pairs={{0,7},{1,8},{2,9},{3,10},{4,11},{5,12},{6,13},{7,14},{8,15},{9,0},... | collective-permute-start | bytes 36872 | tf_op jit(solution)/shard_map/ppermute | solution.py:31
  318.5 8.2 %collective-permute-start.7 = (f32[8,3,128]{2,0,1:T(8,128)S(1)}, f32[8,3,128]{2,0,1:T(8,128)S(1)}, u32[]{:S(2)}, u32[]{:S(2)}) collective-permute-start(f32[8,3,128]{2,0,1:T(8,128)S(1)} %get-tuple-element.149), channel_id=1, source_target_pairs={{0,8},{1,9},{2,10},{3,11},{4,12},{5,13},{6,14},{7,15},{8,0},{9,1},... | collective-permute-start | bytes 36872 | tf_op jit(solution)/shard_map/ppermute | solution.py:31
  320.5 6.5 %collective-permute-start.8 = (f32[8,3,128]{2,0,1:T(8,128)S(1)}, f32[8,3,128]{2,0,1:T(8,128)S(1)}, u32[]{:S(2)}, u32[]{:S(2)}) collective-permute-start(f32[8,3,128]{2,0,1:T(8,128)S(1)} %get-tuple-element.148), channel_id=1, source_target_pairs={{0,9},{1,10},{2,11},{3,12},{4,13},{5,14},{6,15},{7,0},{8,1},{9,2},... | collective-permute-start | bytes 36872 | tf_op jit(solution)/shard_map/ppermute | solution.py:31
  320.6 8.1 %collective-permute-start.9 = (f32[8,3,128]{2,0,1:T(8,128)S(1)}, f32[8,3,128]{2,0,1:T(8,128)S(1)}, u32[]{:S(2)}, u32[]{:S(2)}) collective-permute-start(f32[8,3,128]{2,0,1:T(8,128)S(1)} %get-tuple-element.147), channel_id=1, source_target_pairs={{0,10},{1,11},{2,12},{3,13},{4,14},{5,15},{6,0},{7,1},{8,2},{9,3},... | collective-permute-start | bytes 36872 | tf_op jit(solution)/shard_map/ppermute | solution.py:31
  322.4 8.9 %collective-permute-start.10 = (f32[8,3,128]{2,0,1:T(8,128)S(1)}, f32[8,3,128]{2,0,1:T(8,128)S(1)}, u32[]{:S(2)}, u32[]{:S(2)}) collective-permute-start(f32[8,3,128]{2,0,1:T(8,128)S(1)} %get-tuple-element.146), channel_id=1, source_target_pairs={{0,11},{1,12},{2,13},{3,14},{4,15},{5,0},{6,1},{7,2},{8,3},{9,4},{... | collective-permute-start | bytes 36872 | tf_op jit(solution)/shard_map/ppermute | solution.py:31
  326.1 5.2 %collective-permute-start.11 = (f32[8,3,128]{2,0,1:T(8,128)S(1)}, f32[8,3,128]{2,0,1:T(8,128)S(1)}, u32[]{:S(2)}, u32[]{:S(2)}) collective-permute-start(f32[8,3,128]{2,0,1:T(8,128)S(1)} %get-tuple-element.145), channel_id=1, source_target_pairs={{0,12},{1,13},{2,14},{3,15},{4,0},{5,1},{6,2},{7,3},{8,4},{9,5},{1... | collective-permute-start | bytes 36872 | tf_op jit(solution)/shard_map/ppermute | solution.py:31
  326.7 4.6 %collective-permute-start.12 = (f32[8,3,128]{2,0,1:T(8,128)S(1)}, f32[8,3,128]{2,0,1:T(8,128)S(1)}, u32[]{:S(2)}, u32[]{:S(2)}) collective-permute-start(f32[8,3,128]{2,0,1:T(8,128)S(1)} %get-tuple-element.144), channel_id=1, source_target_pairs={{0,13},{1,14},{2,15},{3,0},{4,1},{5,2},{6,3},{7,4},{8,5},{9,6},{10... | collective-permute-start | bytes 36872 | tf_op jit(solution)/shard_map/ppermute | solution.py:31
  327.0 4.3 %collective-permute-start.13 = (f32[8,3,128]{2,0,1:T(8,128)S(1)}, f32[8,3,128]{2,0,1:T(8,128)S(1)}, u32[]{:S(2)}, u32[]{:S(2)}) collective-permute-start(f32[8,3,128]{2,0,1:T(8,128)S(1)} %get-tuple-element.143), channel_id=1, source_target_pairs={{0,14},{1,15},{2,0},{3,1},{4,2},{5,3},{6,4},{7,5},{8,6},{9,7},{10,... | collective-permute-start | bytes 36872 | tf_op jit(solution)/shard_map/ppermute | solution.py:31
  328.6 4.1 %collective-permute-start.14 = (f32[8,3,128]{2,0,1:T(8,128)S(1)}, f32[8,3,128]{2,0,1:T(8,128)S(1)}, u32[]{:S(2)}, u32[]{:S(2)}) collective-permute-start(f32[8,3,128]{2,0,1:T(8,128)S(1)} %get-tuple-element.142), channel_id=1, source_target_pairs={{0,15},{1,0},{2,1},{3,2},{4,3},{5,4},{6,5},{7,6},{8,7},{9,8},{10,9... | collective-permute-start | bytes 36872 | tf_op jit(solution)/shard_map/ppermute | solution.py:31
Sparse Core Ops, SparseCore 0:
  10.8 54.9 all-gather.1
